TPU v7x, 256 devices: a whole 4x4x8 slice. The times are simulated.
256 devices in a mesh: fsdp: 16 (over y, x), tensor: 16 (over z, core).
Axes of the slice: x: 4, y: 4, z: 8, core: 2. Of those that a mesh axis runs over, the one named last changes fastest.
Arguments:
- inputs: bfloat16 [3072, 8192], P('fsdp'), may hold values from -6 to 6
- cotangent: bfloat16 [3072, 8192], P('fsdp'), may hold values from -1.1953125 to 1.1953125
- up_tiles: bfloat16 [16, 64, 128, 128], P('tensor', 'fsdp'), may hold values from -0.25 to 0.25
- up_rows: int32 [16, 64], P('tensor', 'fsdp'), may hold values from 0 to 63, as said below
- up_cols: int32 [16, 64], P('tensor', 'fsdp'), may hold values from 0 to 15, as said below
- down_tiles: bfloat16 [16, 64, 128, 128], P('tensor', 'fsdp'), may hold values from -0.25 to 0.25
- down_rows: int32 [16, 64], P('tensor', 'fsdp'), may hold values from 0 to 15, as said below
- down_cols: int32 [16, 64], P('tensor', 'fsdp'), may hold values from 0 to 63, as said below
Outputs:
- input_grad: bfloat16 [3072, 8192], P('fsdp', 'tensor')
- up_grad: bfloat16 [16, 64, 128, 128], P('tensor', 'fsdp')
- down_grad: bfloat16 [16, 64, 128, 128], P('tensor', 'fsdp')
Inputs may be any that keep to these rules, and one draw needn't show every extreme that they name: `up_rows`: together with up_cols, the positions of a group's 64 tiles are distinct; slot s is held by fsdp index s // 4. `up_cols`: see up_rows. `down_rows`: together with down_cols, the positions of a group's 64 tiles are distinct; slot s is held by fsdp index s // 4. `down_cols`: see down_rows.
All inputs are finite; a program needn't handle non-finite values.
Results may differ from a plain program's by a relative error of at most 0.015.
Values may be sent and summed in bfloat16 or wider, within the bound.
A program may use at most 128 MiB of HBM per device.

v0:
```python
import jax
import jax.numpy as jnp
from jax import lax
from jax.sharding import PartitionSpec as P

FF = 32768
TILE = 128


def gelu_parts(pre):
    coef = 0.7978845608028654
    inner = coef * (pre + 0.044715 * pre * pre * pre)
    tanh_val = jnp.tanh(inner)
    act = 0.5 * pre * (1.0 + tanh_val)
    slope = 0.5 * (1.0 + tanh_val) + 0.5 * pre * (1.0 - tanh_val * tanh_val) * coef * (
        1.0 + 3.0 * 0.044715 * pre * pre
    )
    return (act, slope)


def on_device(inputs, cotangent, up_tiles, up_rows, up_cols, down_tiles, down_rows, down_cols):
    tok_count = inputs.shape[0]
    row_blocks = inputs.shape[1] // TILE
    group_cols = FF // (lax.axis_size("tensor") * TILE)
    input_blocks = inputs.reshape(tok_count, row_blocks, TILE)
    cotan_blocks = cotangent.reshape(tok_count, row_blocks, TILE)
    gathered = (
        lax.all_gather(up_tiles, "fsdp", axis=1, tiled=True),
        lax.all_gather(up_rows, "fsdp", axis=1, tiled=True),
        lax.all_gather(up_cols, "fsdp", axis=1, tiled=True),
        lax.all_gather(down_tiles, "fsdp", axis=1, tiled=True),
        lax.all_gather(down_rows, "fsdp", axis=1, tiled=True),
        lax.all_gather(down_cols, "fsdp", axis=1, tiled=True),
    )
    w_up, r_up, c_up = (gathered[0][0], gathered[1][0], gathered[2][0])
    w_down, r_down, c_down = (gathered[3][0], gathered[4][0], gathered[5][0])
    x_sel = jnp.take(input_blocks, r_up, axis=1)
    prod = jnp.einsum("tsk,skf->stf", x_sel, w_up, preferred_element_type=jnp.float32)
    pre = jax.ops.segment_sum(prod, c_up, num_segments=group_cols)
    act, slope = gelu_parts(pre)
    hidden = act.astype(jnp.bfloat16)
    dy_sel = jnp.take(cotan_blocks, c_down, axis=1)
    h_sel = jnp.take(hidden, r_down, axis=0)
    back = jnp.einsum("tsk,sfk->stf", dy_sel, w_down, preferred_element_type=jnp.float32)
    dhid = jax.ops.segment_sum(back, r_down, num_segments=group_cols)
    dpre = (dhid * slope).astype(jnp.bfloat16)
    dp_sel = jnp.take(dpre, c_up, axis=0)
    both_sum = lax.psum_scatter(
        jnp.stack(
            [
                jnp.einsum("tsk,stf->skf", x_sel, dp_sel, preferred_element_type=jnp.float32),
                jnp.einsum("stf,tsk->sfk", h_sel, dy_sel, preferred_element_type=jnp.float32),
            ],
            axis=1,
        ).astype(jnp.bfloat16),
        "fsdp",
        scatter_dimension=0,
        tiled=True,
    ).astype(jnp.float32)
    up_sum = both_sum[:, 0]
    down_sum = both_sum[:, 1]
    back_in = jnp.einsum("stf,skf->stk", dp_sel, w_up, preferred_element_type=jnp.float32)
    in_part = jax.ops.segment_sum(back_in, r_up, num_segments=row_blocks)
    own_blocks = lax.psum_scatter(
        in_part.astype(jnp.bfloat16), "tensor", scatter_dimension=0, tiled=True
    ).astype(jnp.float32)
    input_grad = jnp.transpose(own_blocks, (1, 0, 2)).reshape(tok_count, -1).astype(jnp.bfloat16)
    up_grad = up_sum.astype(jnp.bfloat16)[None]
    down_grad = down_sum.astype(jnp.bfloat16)[None]
    return (input_grad, up_grad, down_grad)


def solution(mesh):
    placed = (
        P("fsdp", None),
        P("fsdp", None),
        P("tensor", "fsdp", None, None),
        P("tensor", "fsdp"),
        P("tensor", "fsdp"),
        P("tensor", "fsdp", None, None),
        P("tensor", "fsdp"),
        P("tensor", "fsdp"),
    )
    return jax.shard_map(
        on_device,
        mesh=mesh,
        in_specs=placed,
        out_specs=(
            P("fsdp", "tensor"),
            P("tensor", "fsdp", None, None),
            P("tensor", "fsdp", None, None),
        ),
        check_vma=False,
    )
```

profile of v0, /device:TPU:2, one launch (start us, length us, event | category | flops | bytes accessed | tf_op | source)
XLA Modules:
  0.0 336.9 jit_solution(617230634421711850)
XLA Ops:
  8.0 0.7 all-gather.3.cloned.1.call-update
  8.7 1.3 fusion.33
  10.7 0.8 bitcast_dynamic-update-slice_fusion
  11.5 0.7 bitcast_dynamic-update-slice_fusion.1
  12.2 0.7 bitcast_dynamic-update-slice_fusion.2
  13.0 0.7 bitcast_dynamic-update-slice_fusion.3
  13.7 15.6 %all-reduce.5 = (s32[64]{0:T(128)S(1)}, s32[64]{0:T(128)S(1)}, s32[64]{0:T(128)S(1)}, s32[64]{0:T(128)S(1)}) all-reduce(s32[64]{0:T(128)S(1)} %bitcast_dynamic-update-slice_fusion.3, s32[64]{0:T(128)S(1)} %bitcast_dynamic-update-slice_fusion.1, s32[64]{0:T(128)S(1)} %bitcast_dynamic-update-slice_fusion, ...), channel_id=1, replica_groups=mesh['fsdp'=16,'tensor'=16] {'fsdp'}, use_global_device_ids=true, to_apply=%add | all-reduce | flops 256 | bytes 2048 | tf_op jit(solution)/shard_map/broadcast_in_dim;squeeze | solution.py:63
  29.4 2.5 copy_bitcast_fusion
  31.9 4.5 %gather_fusion.1 = bf16[64,192,128]{2,1,0:T(8,128)(2,1)} fusion(bf16[192,64,128]{2,0,1:T(8,128)(2,1)} %copy_bitcast_fusion, s32[1024]{0:T(1024)S(1)} %pad_clamp_fusion.2), kind=kCustom, calls=%fused_computation.2.clone | custom fusion | bytes 6291712 | tf_op jit(solution)/shard_map/jit(_take)/gather | solution.py:37
  36.4 2.8 copy_bitcast_fusion.1
  39.2 2.6 gather_fusion
  41.9 21.2 %all-gather.5.cloned.1.call-done = bf16[1,64,128,128]{3,2,0,1:T(8,128)(2,1)} async-done(((bf16[1,4,128,128]{3,2,0,1:T(8,128)(2,1)}), bf16[1,64,128,128]{3,2,0,1:T(8,128)(2,1)}) %all-gather.5.cloned.1.call-update) | async-done | bytes 2097168 | tf_op jit(solution)/shard_map/all_gather | solution.py:28
  63.1 6.2 %fusion.2 = f32[64,192,128]{2,1,0:T(8,128)} fusion(bf16[1,64,128,128]{3,2,0,1:T(8,128)(2,1)} %all-gather.5.cloned.1.call-done, bf16[64,192,128]{2,1,0:T(8,128)(2,1)} %gather_fusion.1, pred[64]{0:T(512)(128)(4,1)S(1)} %get-tuple-element.18), kind=kOutput, calls=%fused_computation.12 | convolution fusion | flops 404226048 | bytes 11534400 | tf_op jit(solution)/shard_map/tsk,skf->stf/dot_general | solution.py:38
  69.4 10.9 %scatter_fusion.1 = f32[16,192,128]{2,1,0:T(8,128)S(1)} fusion(f32[16,192,128]{2,1,0:T(8,128)S(1)} %broadcast.18.clone, s32[64]{0:T(128)S(1)} %get-tuple-element.8, f32[64,192,128]{2,1,0:T(8,128)} %fusion.2), kind=kCustom, calls=%fused_computation.5 | custom fusion | flops 1572864 | bytes 18874624 | tf_op jit(solution)/shard_map/scatter-add | solution.py:39
  80.3 34.6 %all-gather.3.cloned.1.call-done = bf16[1,64,128,128]{3,2,0,1:T(8,128)(2,1)} async-done(((bf16[1,4,128,128]{3,2,0,1:T(8,128)(2,1)}), bf16[1,64,128,128]{3,2,0,1:T(8,128)(2,1)}) %all-gather.3.cloned.1.call-update) | async-done | bytes 2097168 | tf_op jit(solution)/shard_map/all_gather | solution.py:31
  114.9 6.7 %fusion.6 = f32[64,192,128]{2,1,0:T(8,128)} fusion(bf16[1,64,128,128]{3,2,0,1:T(8,128)(2,1)} %all-gather.3.cloned.1.call-done, bf16[64,192,128]{2,1,0:T(8,128)(2,1)} %gather_fusion, pred[64]{0:T(512)(128)(4,1)S(1)} %compare_and_fusion.3), kind=kOutput, calls=%fused_computation.16 | convolution fusion | flops 404226048 | bytes 11534400 | tf_op jit(solution)/shard_map/tsk,sfk->stf/dot_general | solution.py:44
  121.7 10.6 %scatter_fusion = f32[16,192,128]{2,1,0:T(8,128)S(1)} fusion(f32[16,192,128]{2,1,0:T(8,128)S(1)} %broadcast.18.clone.1, s32[64]{0:T(128)S(1)} %get-tuple-element.6, f32[64,192,128]{2,1,0:T(8,128)} %fusion.6), kind=kCustom, calls=%fused_computation.4 | custom fusion | flops 1572864 | bytes 18874624 | tf_op jit(solution)/shard_map/scatter-add | solution.py:45
  132.4 2.3 multiply_convert_fusion
  134.7 3.7 %gather_fusion.2 = bf16[64,192,128]{2,1,0:T(8,128)(2,1)} fusion(bf16[16,192,128]{2,1,0:T(8,128)(2,1)} %get-tuple-element.12, s32[1024]{0:T(1024)S(1)} %pad_clamp_fusion.1), kind=kCustom, calls=%fused_computation.1.clone | custom fusion | bytes 6291712 | tf_op jit(solution)/shard_map/jit(_take)/gather | solution.py:47
  138.4 4.5 %convert_bitcast_fusion.1 = bf16[64,1,128,128]{3,2,0,1:T(8,128)(2,1)S(1)} fusion(bf16[64,192,128]{2,1,0:T(8,128)(2,1)} %gather_fusion.1, pred[64]{0:T(512)(128)(4,1)S(1)} %get-tuple-element.18, bf16[64,192,128]{2,1,0:T(8,128)(2,1)} %gather_fusion.2, pred[64]{0:T(512)(128)(4,1)S(1)} %get-tuple-element.17), kind=kOutput, calls=%fused_computation.30 | convolution fusion | flops 406847488 | bytes 8388736 | tf_op jit(solution)/shard_map/tsk,stf->skf/dot_general | solution.py:51
  142.9 2.6 gather_fusion.3
  145.5 4.4 %convert_bitcast_fusion = bf16[64,1,128,128]{3,2,0,1:T(8,128)(2,1)S(1)} fusion(bf16[64,192,128]{2,1,0:T(8,128)(2,1)} %gather_fusion.3, pred[64]{0:T(512)(128)(4,1)S(1)} %compare_and_fusion, bf16[64,192,128]{2,1,0:T(8,128)(2,1)} %gather_fusion, pred[64]{0:T(512)(128)(4,1)S(1)} %compare_and_fusion.3), kind=kOutput, calls=%fused_computation.29 | convolution fusion | flops 406847488 | bytes 8388736 | tf_op jit(solution)/shard_map/stf,tsk->sfk/dot_general | solution.py:52
  149.9 2.3 pad_maximum_fusion
  152.3 1.8 copy-done.3
  154.1 5.7 %fusion.10 = f32[64,192,128]{2,1,0:T(8,128)} fusion(bf16[1,64,128,128]{3,2,0,1:T(8,128)(2,1)} %all-gather.5.cloned.1.call-done, bf16[64,192,128]{2,1,0:T(8,128)(2,1)S(1)} %copy-done.3, pred[64]{0:T(512)(128)(4,1)S(1)} %get-tuple-element.17), kind=kOutput, calls=%fused_computation.25 | convolution fusion | flops 404226048 | bytes 11534400 | tf_op jit(solution)/shard_map/stf,skf->stk/dot_general | solution.py:62
  159.8 3.6 %broadcast_in_dim.23 = f32[64,192,128]{2,1,0:T(8,128)} broadcast(f32[]{:T(128)} %constant.22.clone.1), dimensions={} | broadcast | bytes 6291460 | tf_op jit(solution)/shard_map/broadcast_in_dim | solution.py:63
  163.4 16.8 %scatter_fusion.2 = f32[64,192,128]{2,1,0:T(8,128)} fusion(f32[64,192,128]{2,1,0:T(8,128)} %broadcast_in_dim.23, s32[64]{0:T(128)S(1)} %get-tuple-element.5, f32[64,192,128]{2,1,0:T(8,128)} %fusion.10), kind=kCustom, calls=%fused_computation.6 | custom fusion | flops 1572864 | bytes 18874624 | tf_op jit(solution)/shard_map/scatter-add | solution.py:63
  180.2 5.3 %convert_element_type.42 = bf16[64,192,128]{2,1,0:T(8,128)(2,1)} convert(f32[64,192,128]{2,1,0:T(8,128)} %scatter_fusion.2) | non-fusion elementwise | flops 1572864 | bytes 9437184 | tf_op jit(solution)/shard_map/convert_element_type | solution.py:65
  186.2 79.6 %all-reduce.8.cloned.1.call-done = bf16[64,2,128,128]{3,2,0,1:T(8,128)(2,1)} async-done(((bf16[64,2,128,128]{3,2,0,1:T(8,128)(2,1)}), bf16[64,2,128,128]{3,2,0,1:T(8,128)(2,1)}) %all-reduce.8.cloned.1.call-update) | async-done | bytes 4194320
  265.8 1.7 dynamic-slice_bitcast_fusion
  267.4 61.4 %reduce-scatter.5.cloned.1.call-done = bf16[4,192,128]{2,1,0:T(8,128)(2,1)} async-done(((bf16[64,192,128]{2,1,0:T(8,128)(2,1)}), bf16[4,192,128]{2,1,0:T(8,128)(2,1)}) %reduce-scatter.5.cloned.1.call-update) | async-done | bytes 196624 | tf_op jit(solution)/shard_map/reduce_scatter | solution.py:64
  328.8 1.6 copy_bitcast_fusion.2
  (30 shorter events, 1.3 us)
Async XLA Ops:
  7.2 22.2 %copy-start = (bf16[192,8192]{1,0:T(8,128)(2,1)S(1)}, bf16[192,8192]{1,0:T(8,128)(2,1)}, u32[]{:S(2)}) copy-start(bf16[192,8192]{1,0:T(8,128)(2,1)} %param.12) | copy-start | bytes 9437188
  7.2 55.9 %all-gather.5.cloned.1.call-start = ((), (), s32[]{:S(2)}) async-start(), calls=%async_computation.2 | async-start | bytes 2228224 | tf_op jit(solution)/shard_map/all_gather | solution.py:28
  7.9 107.0 %all-gather.3.cloned.1.call-start = ((), (), s32[]{:S(2)}) async-start(), calls=%async_computation.1 | async-start | bytes 2228224 | tf_op jit(solution)/shard_map/all_gather | solution.py:31
  8.7 257.1 %all-reduce.8.cloned.1.call-start = ((), (), s32[]{:S(2)}) async-start(), calls=%async_computation.4 | async-start | bytes 8388608
  138.4 4.5 %copy-start.2 = (bf16[16,192,128]{2,1,0:T(8,128)(2,1)S(1)}, bf16[16,192,128]{2,1,0:T(8,128)(2,1)}, u32[]{:S(2)}) copy-start(bf16[16,192,128]{2,1,0:T(8,128)(2,1)} %get-tuple-element.11) | copy-start | bytes 2359300
  152.2 1.9 copy-start.3
  152.2 176.6 %reduce-scatter.5.cloned.1.call-start = ((), (), s32[]{:S(2)}) async-start(), calls=%async_computation.3 | async-start | bytes 3342336 | tf_op jit(solution)/shard_map/reduce_scatter | solution.py:64
  180.2 150.2 %copy-start.1 = (bf16[192,8192]{1,0:T(8,128)(2,1)S(1)}, bf16[192,8192]{1,0:T(8,128)(2,1)}, u32[]{:S(2)}) copy-start(bf16[192,8192]{1,0:T(8,128)(2,1)} %param.12) | copy-start | bytes 9437188
Sparse Core Ops, SparseCore 0:
  10.4 52.5 all-gather.4
  65.5 49.3 all-gather.2
  152.3 113.3 all-reduce.7
  268.2 60.5 reduce-scatter.4
where the time goes:
time: 338 us; the launch traced here: 337 us
  waiting for transfers between devices  198 us (59%)
  other arithmetic  48.2 us (14%)
  local copies, waits for them, and re-layouts  32.1 us (9%)
  matrix products  27.5 us (8%)
  blocking collectives  15.6 us (5%)
  between operations  15.2 us (4%)
    unnamed x5, waiting for transfers between devices  81 us
    reduce_scatter x1, waiting for transfers between devices, on_device(): lax.psum_scatter(in_part.astype(jnp.bfloat16), 'tensor', scatter_dimensio...  61.4 us
    all_gather x1, waiting for transfers between devices, on_device(): lax.all_gather(down_tiles, 'fsdp', axis=1, tiled=True)  34.6 us
    all_gather x1, waiting for transfers between devices, on_device(): lax.all_gather(up_tiles, 'fsdp', axis=1, tiled=True)  21.2 us
    scatter-add x1, other arithmetic, on_device(): in_part = jax.ops.segment_sum(back_in, r_up, num_segments=row_blocks)  16.8 us
    another operation x1, blocking collectives, on_device(): in_part = jax.ops.segment_sum(back_in, r_up, num_segments=row_blocks)  15.6 us
    scatter-add x1, other arithmetic, on_device(): pre = jax.ops.segment_sum(prod, c_up, num_segments=group_cols)  10.9 us
    scatter-add x1, other arithmetic, on_device(): dhid = jax.ops.segment_sum(back, r_down, num_segments=group_cols)  10.6 us
  transfers between devices with their start and end apart: 4, of which 4 were waited for; matrix products, arithmetic and copies ran while one was open for 20% of the time, Pallas kernels for 0%

commit v1 on v0

--- a/solution.py
+++ b/solution.py
@@ -25,7 +25,9 @@
     input_blocks = inputs.reshape(tok_count, row_blocks, TILE)
     cotan_blocks = cotangent.reshape(tok_count, row_blocks, TILE)
     gathered = (
-        lax.all_gather(up_tiles, "fsdp", axis=1, tiled=True),
+        jnp.concatenate(
+            lax.all_to_all(jnp.stack([up_tiles] * lax.axis_size("fsdp")), "fsdp", 0, 0), axis=1
+        ),
         lax.all_gather(up_rows, "fsdp", axis=1, tiled=True),
         lax.all_gather(up_cols, "fsdp", axis=1, tiled=True),
         lax.all_gather(down_tiles, "fsdp", axis=1, tiled=True),

time: 338 us -> 310 us (0.917)
  waiting for transfers between devices: 198 us -> 143 us
  blocking collectives: 15.6 us -> 36.4 us
  starting transfers between devices: 0.16 us -> 7.59 us
    all_gather x1, waiting for transfers between devices: 34.6 us -> 0.02 us  [on_device(): lax.all_gather(down_tiles, 'fsdp', axis=1, tiled=True)]
    all_gather x1 -> x0, waiting for transfers between devices: 21.2 us -> none  [on_device(): lax.all_gather(up_tiles, 'fsdp', axis=1, tiled=True)]
    another operation x1, blocking collectives: 15.6 us -> 36.4 us  [on_device(): in_part = jax.ops.segment_sum(back_in, r_up, num_segments=row_blocks)]
    all_to_all x0 -> x1, starting transfers between devices: none -> 7.48 us  [on_device(): lax.all_to_all(jnp.stack([up_tiles] * lax.axis_size('fsdp')), 'fsdp', 0, 0)]
    unnamed x5 -> x4, waiting for transfers between devices: 81 us -> 81.1 us
  transfers between devices with their start and end apart: 4 -> 4, of which waited for: 4 -> 2; matrix products, arithmetic and copies ran while one was open for 20% -> 21% of each run, Pallas kernels for 0% -> 0%
where the time goes in v1:
time: 310 us; the launch traced here: 309 us
  waiting for transfers between devices  143 us (46%)
  other arithmetic  48.1 us (16%)
  blocking collectives  36.4 us (12%)
  local copies, waits for them, and re-layouts  31.5 us (10%)
  matrix products  27.7 us (9%)
  between operations  15.3 us (5%)
  starting transfers between devices  7.59 us (2%)
    unnamed x4, waiting for transfers between devices  81.1 us
    reduce_scatter x1, waiting for transfers between devices, on_device(): lax.psum_scatter(in_part.astype(jnp.bfloat16), 'tensor', scatter_dimensio...  61.5 us
    another operation x1, blocking collectives, on_device(): in_part = jax.ops.segment_sum(back_in, r_up, num_segments=row_blocks)  36.4 us
    scatter-add x1, other arithmetic, on_device(): in_part = jax.ops.segment_sum(back_in, r_up, num_segments=row_blocks)  16.8 us
    scatter-add x1, other arithmetic, on_device(): pre = jax.ops.segment_sum(prod, c_up, num_segments=group_cols)  10.8 us
    scatter-add x1, other arithmetic, on_device(): dhid = jax.ops.segment_sum(back, r_down, num_segments=group_cols)  10.6 us
    all_to_all x1, starting transfers between devices, on_device(): lax.all_to_all(jnp.stack([up_tiles] * lax.axis_size('fsdp')), 'fsdp', 0, 0)  7.48 us
    dot_general x1, matrix products, on_device(): jnp.einsum('tsk,sfk->stf', dy_sel, w_down, preferred_element_type=jnp.flo...  6.72 us
  transfers between devices with their start and end apart: 4, of which 2 were waited for; matrix products, arithmetic and copies ran while one was open for 21% of the time, Pallas kernels for 0%

profile of v1, /device:TPU:2, one launch (start us, length us, event | category | flops | bytes accessed | tf_op | source)
XLA Modules:
  0.0 309.2 jit_solution(11609422963560149094)
XLA Ops:
  7.2 2.9 stack.11
  10.2 7.5 %all-to-all-start = ((bf16[16,1,4,128,128]{4,3,2,1,0:T(8,128)(2,1)}), bf16[16,1,4,128,128]{4,3,2,1,0:T(8,128)(2,1)}, u32[]{:S(2)}, u32[]{:S(2)}) async-start(bf16[16,1,4,128,128]{4,3,2,1,0:T(8,128)(2,1)} %stack.11), calls=%async_computation | async-start | bytes 4194304 | tf_op jit(solution)/shard_map/all_to_all | solution.py:29
  17.7 0.7 all-gather.2.cloned.1.call-update
  18.4 0.6 fusion.31
  19.7 0.1 bitcast_dynamic-update-slice_fusion
  19.8 0.1 bitcast_dynamic-update-slice_fusion.1
  20.1 36.4 %all-reduce.5 = (s32[64]{0:T(128)S(1)}, s32[64]{0:T(128)S(1)}, s32[64]{0:T(128)S(1)}, s32[64]{0:T(128)S(1)}) all-reduce(s32[64]{0:T(128)S(1)} %bitcast_dynamic-update-slice_fusion.3, s32[64]{0:T(128)S(1)} %bitcast_dynamic-update-slice_fusion.1, s32[64]{0:T(128)S(1)} %bitcast_dynamic-update-slice_fusion, ...), channel_id=1, replica_groups=mesh['fsdp'=16,'tensor'=16] {'fsdp'}, use_global_device_ids=true, to_apply=%add | all-reduce | flops 256 | bytes 2048 | tf_op jit(solution)/shard_map/broadcast_in_dim;squeeze | solution.py:65
  56.5 2.5 copy_bitcast_fusion
  59.0 4.5 %gather_fusion.1 = bf16[64,192,128]{2,1,0:T(8,128)(2,1)} fusion(bf16[192,64,128]{2,0,1:T(8,128)(2,1)} %copy_bitcast_fusion, s32[1024]{0:T(1024)S(1)} %pad_clamp_fusion.2), kind=kCustom, calls=%fused_computation.2.clone | custom fusion | bytes 6291712 | tf_op jit(solution)/shard_map/jit(_take)/gather | solution.py:39
  63.5 2.8 copy_bitcast_fusion.1
  66.3 2.7 gather_fusion
  69.1 6.3 %fusion.2 = f32[64,192,128]{2,1,0:T(8,128)} fusion(bf16[64,128,128]{2,1,0:T(8,128)(2,1)} %bitcast.10, bf16[64,192,128]{2,1,0:T(8,128)(2,1)} %gather_fusion.1, pred[64]{0:T(512)(128)(4,1)S(1)} %get-tuple-element.18), kind=kOutput, calls=%fused_computation.12 | convolution fusion | flops 404226048 | bytes 11534400 | tf_op jit(solution)/shard_map/tsk,skf->stf/dot_general | solution.py:40
  75.4 0.1 broadcast.21.clone
  75.6 10.8 %scatter_fusion.1 = f32[16,192,128]{2,1,0:T(8,128)S(1)} fusion(f32[16,192,128]{2,1,0:T(8,128)S(1)} %broadcast.21.clone, s32[64]{0:T(128)S(1)} %get-tuple-element.8, f32[64,192,128]{2,1,0:T(8,128)} %fusion.2), kind=kCustom, calls=%fused_computation.5 | custom fusion | flops 1572864 | bytes 18874624 | tf_op jit(solution)/shard_map/scatter-add | solution.py:41
  86.4 6.7 %fusion.6 = f32[64,192,128]{2,1,0:T(8,128)} fusion(bf16[1,64,128,128]{3,2,0,1:T(8,128)(2,1)} %all-gather.2.cloned.1.call-done, bf16[64,192,128]{2,1,0:T(8,128)(2,1)} %gather_fusion, pred[64]{0:T(512)(128)(4,1)S(1)} %compare_and_fusion.3), kind=kOutput, calls=%fused_computation.16 | convolution fusion | flops 404226048 | bytes 11534400 | tf_op jit(solution)/shard_map/tsk,sfk->stf/dot_general | solution.py:46
  93.1 0.1 broadcast.21.clone.1
  93.3 10.6 %scatter_fusion = f32[16,192,128]{2,1,0:T(8,128)S(1)} fusion(f32[16,192,128]{2,1,0:T(8,128)S(1)} %broadcast.21.clone.1, s32[64]{0:T(128)S(1)} %get-tuple-element.6, f32[64,192,128]{2,1,0:T(8,128)} %fusion.6), kind=kCustom, calls=%fused_computation.4 | custom fusion | flops 1572864 | bytes 18874624 | tf_op jit(solution)/shard_map/scatter-add | solution.py:47
  103.9 2.3 multiply_convert_fusion
  106.2 3.7 %gather_fusion.2 = bf16[64,192,128]{2,1,0:T(8,128)(2,1)} fusion(bf16[16,192,128]{2,1,0:T(8,128)(2,1)} %get-tuple-element.12, s32[1024]{0:T(1024)S(1)} %pad_clamp_fusion.1), kind=kCustom, calls=%fused_computation.1.clone | custom fusion | bytes 6291712 | tf_op jit(solution)/shard_map/jit(_take)/gather | solution.py:49
  109.9 4.5 %convert_bitcast_fusion.1 = bf16[64,1,128,128]{3,2,0,1:T(8,128)(2,1)S(1)} fusion(bf16[64,192,128]{2,1,0:T(8,128)(2,1)} %gather_fusion.1, pred[64]{0:T(512)(128)(4,1)S(1)} %get-tuple-element.18, bf16[64,192,128]{2,1,0:T(8,128)(2,1)} %gather_fusion.2, pred[64]{0:T(512)(128)(4,1)S(1)} %get-tuple-element.17), kind=kOutput, calls=%fused_computation.27 | convolution fusion | flops 406847488 | bytes 8388736 | tf_op jit(solution)/shard_map/tsk,stf->skf/dot_general | solution.py:53
  114.4 2.6 gather_fusion.3
  117.1 4.4 %convert_bitcast_fusion = bf16[64,1,128,128]{3,2,0,1:T(8,128)(2,1)S(1)} fusion(bf16[64,192,128]{2,1,0:T(8,128)(2,1)} %gather_fusion.3, pred[64]{0:T(512)(128)(4,1)S(1)} %compare_and_fusion, bf16[64,192,128]{2,1,0:T(8,128)(2,1)} %gather_fusion, pred[64]{0:T(512)(128)(4,1)S(1)} %compare_and_fusion.3), kind=kOutput, calls=%fused_computation.26 | convolution fusion | flops 406847488 | bytes 8388736 | tf_op jit(solution)/shard_map/stf,tsk->sfk/dot_general | solution.py:54
  121.5 2.3 pad_maximum_fusion
  123.8 1.8 copy-done.3
  125.7 5.8 %fusion.25 = f32[64,192,128]{2,1,0:T(8,128)} fusion(bf16[64,128,128]{2,1,0:T(8,128)(2,1)} %bitcast.10, bf16[64,192,128]{2,1,0:T(8,128)(2,1)S(1)} %copy-done.3, pred[64]{0:T(512)(128)(4,1)S(1)} %get-tuple-element.17), kind=kOutput, calls=%fused_computation.37 | convolution fusion | flops 404226048 | bytes 11534400 | tf_op jit(solution)/shard_map/stf,skf->stk/dot_general | solution.py:64
  131.4 3.4 %broadcast_in_dim.23 = f32[64,192,128]{2,1,0:T(8,128)} broadcast(f32[]{:T(128)} %constant.22.clone.1), dimensions={} | broadcast | bytes 6291460 | tf_op jit(solution)/shard_map/broadcast_in_dim | solution.py:65
  134.8 16.8 %scatter_fusion.2 = f32[64,192,128]{2,1,0:T(8,128)} fusion(f32[64,192,128]{2,1,0:T(8,128)} %broadcast_in_dim.23, s32[64]{0:T(128)S(1)} %get-tuple-element.5, f32[64,192,128]{2,1,0:T(8,128)} %fusion.25), kind=kCustom, calls=%fused_computation.6 | custom fusion | flops 1572864 | bytes 18874624 | tf_op jit(solution)/shard_map/scatter-add | solution.py:65
  151.6 5.3 %convert_element_type.42 = bf16[64,192,128]{2,1,0:T(8,128)(2,1)} convert(f32[64,192,128]{2,1,0:T(8,128)} %scatter_fusion.2) | non-fusion elementwise | flops 1572864 | bytes 9437184 | tf_op jit(solution)/shard_map/convert_element_type | solution.py:67
  157.5 80.4 %all-reduce.8.cloned.1.call-done = bf16[64,2,128,128]{3,2,0,1:T(8,128)(2,1)} async-done(((bf16[64,2,128,128]{3,2,0,1:T(8,128)(2,1)}), bf16[64,2,128,128]{3,2,0,1:T(8,128)(2,1)}) %all-reduce.8.cloned.1.call-update) | async-done | bytes 4194320
  237.9 1.7 dynamic-slice_bitcast_fusion
  239.6 61.5 %reduce-scatter.5.cloned.1.call-done = bf16[4,192,128]{2,1,0:T(8,128)(2,1)} async-done(((bf16[64,192,128]{2,1,0:T(8,128)(2,1)}), bf16[4,192,128]{2,1,0:T(8,128)(2,1)}) %reduce-scatter.5.cloned.1.call-update) | async-done | bytes 196624 | tf_op jit(solution)/shard_map/reduce_scatter | solution.py:66
  301.1 1.6 copy_bitcast_fusion.2
  (40 shorter events, 0.5 us)
Async XLA Ops:
  7.2 49.3 %copy-start = (bf16[192,8192]{1,0:T(8,128)(2,1)S(1)}, bf16[192,8192]{1,0:T(8,128)(2,1)}, u32[]{:S(2)}) copy-start(bf16[192,8192]{1,0:T(8,128)(2,1)} %param.12) | copy-start | bytes 9437188
  7.2 11.2 %copy-start.4 = (u32[256]{0:T(256)S(1)}, u32[256]{0:T(256)}, u32[]{:S(2)}) copy-start(u32[256]{0:T(256)} %constant.41) | copy-start | bytes 3076
  7.2 12.5 %copy-start.5 = (s32[1,4]{1,0:T(1,128)S(1)}, s32[1,4]{1,0:T(1,128)}, u32[]{:S(2)}) copy-start(s32[1,4]{1,0:T(1,128)} %param.19) | copy-start | bytes 52
  7.2 12.6 %copy-start.6 = (s32[1,4]{1,0:T(1,128)S(1)}, s32[1,4]{1,0:T(1,128)}, u32[]{:S(2)}) copy-start(s32[1,4]{1,0:T(1,128)} %param.18) | copy-start | bytes 52
  7.2 12.7 %copy-start.7 = (s32[1,4]{1,0:T(1,128)S(1)}, s32[1,4]{1,0:T(1,128)}, u32[]{:S(2)}) copy-start(s32[1,4]{1,0:T(1,128)} %param.16) | copy-start | bytes 52
  7.2 12.8 %copy-start.8 = (s32[1,4]{1,0:T(1,128)S(1)}, s32[1,4]{1,0:T(1,128)}, u32[]{:S(2)}) copy-start(s32[1,4]{1,0:T(1,128)} %param.15) | copy-start | bytes 52
  10.2 58.9 %all-to-all-start = ((bf16[16,1,4,128,128]{4,3,2,1,0:T(8,128)(2,1)}), bf16[16,1,4,128,128]{4,3,2,1,0:T(8,128)(2,1)}, u32[]{:S(2)}, u32[]{:S(2)}) async-start(bf16[16,1,4,128,128]{4,3,2,1,0:T(8,128)(2,1)} %stack.11), calls=%async_computation | async-start | bytes 4194304 | tf_op jit(solution)/shard_map/all_to_all | solution.py:29
  17.6 68.8 %all-gather.2.cloned.1.call-start = ((), (), s32[]{:S(2)}) async-start(), calls=%async_computation.2 | async-start | bytes 2228224 | tf_op jit(solution)/shard_map/all_gather | solution.py:33
  18.4 219.5 %all-reduce.8.cloned.1.call-start = ((), (), s32[]{:S(2)}) async-start(), calls=%async_computation.4 | async-start | bytes 8388608
  109.9 4.5 %copy-start.2 = (bf16[16,192,128]{2,1,0:T(8,128)(2,1)S(1)}, bf16[16,192,128]{2,1,0:T(8,128)(2,1)}, u32[]{:S(2)}) copy-start(bf16[16,192,128]{2,1,0:T(8,128)(2,1)} %get-tuple-element.11) | copy-start | bytes 2359300
  123.8 1.9 copy-start.3
  123.8 177.3 %reduce-scatter.5.cloned.1.call-start = ((), (), s32[]{:S(2)}) async-start(), calls=%async_computation.3 | async-start | bytes 3342336 | tf_op jit(solution)/shard_map/reduce_scatter | solution.py:66
  151.6 151.1 %copy-start.1 = (bf16[192,8192]{1,0:T(8,128)(2,1)S(1)}, bf16[192,8192]{1,0:T(8,128)(2,1)}, u32[]{:S(2)}) copy-start(bf16[192,8192]{1,0:T(8,128)(2,1)} %param.12) | copy-start | bytes 9437188
Sparse Core Ops, SparseCore 0:
  20.9 58.6 all-gather.1
  123.9 113.9 all-reduce.7
  240.4 60.5 reduce-scatter.4
